TPU v7x, 768 devices: a whole 4x8x12 slice. The times are simulated.
768 devices in a mesh: ctx: 32 (over x, y), tp: 8 (over z_lo, core), grp: 3 (over z_hi).
Axes of the slice: x: 4, y: 8, z: 12 (z_hi: 3, z_lo: 4; z = z_hi * 4 + z_lo), core: 2. Of those that a mesh axis runs over, the one named last changes fastest.
Arguments:
- outer_gate: bfloat16 [12288, 8192], P(('ctx', 'grp'), 'tp'), may hold values from -60 to 60
- inner_gate: bfloat16 [12288, 8192], P(('ctx', 'grp'), 'tp'), may hold values from -6 to 6
- signal: bfloat16 [12288, 8192], P(('ctx', 'grp'), 'tp'), may hold values from -6 to 6
- residues: float32 [16, 8192], P(None, 'tp'), may hold values from -4 to 4
- log_rates: float32 [16, 8192], P(None, 'tp'), as said below
- norm_gain: bfloat16 [8192], P('tp'), may hold values from 0.5 to 1.5
- cotangent: bfloat16 [12288, 8192], P(('ctx', 'grp'), 'tp'), may hold values from -6 to 6
Outputs:
- output: bfloat16 [12288, 8192], P(('ctx', 'grp'), 'tp')
- grad_outer: bfloat16 [12288, 8192], P(('ctx', 'grp'), 'tp')
- grad_inner: bfloat16 [12288, 8192], P(('ctx', 'grp'), 'tp')
- grad_signal: bfloat16 [12288, 8192], P(('ctx', 'grp'), 'tp')
- residue_grads: float32 [16, 8192], P(None, 'tp')
- rate_grads: float32 [16, 8192], P(None, 'tp')
Inputs may be any that keep to these rules, and one draw needn't show every extreme that they name: `log_rates`: each entry is the natural logarithm of a rate between 0.1 / 12288 and 1 / 24.
All inputs are finite; a program needn't handle non-finite values.
Results may differ from a plain program's by a relative error of at most 0.0029.
Values sent between devices are 32-bit elements; how exact they have to be, the bound alone decides.
A program may use at most 64 MiB of HBM per device.

v0:
```python
import math

import jax
import jax.numpy as jnp
from jax import lax
from jax.sharding import PartitionSpec as P

D = 8192


def carried_in(part, axis, combine, identity, reverse):
    count = lax.axis_size(axis)
    place = lax.axis_index(axis)
    ahead = count - 1 - place if reverse else place
    gathered = jax.tree.map(lambda a: lax.all_gather(a, axis), part)
    state = jax.tree.map(lambda a, e: jnp.zeros_like(a) + jnp.asarray(e, a.dtype), part, identity)

    def one(lap, state):
        source = count - 1 - lap if reverse else lap
        return combine(
            state, jax.tree.map(lambda a: lax.dynamic_index_in_dim(a, source, 0, False), gathered)
        )

    return lax.fori_loop(0, ahead, one, state)


def chain(earlier, later):
    return (earlier[0] * later[0], earlier[1] * later[0] + later[1])


def decay_tables(log_rates, block):
    rates = jnp.exp(log_rates)
    lags = jnp.arange(block, dtype=jnp.float32)
    powers = jnp.exp(-rates[:, None, :] * lags[None, :, None])
    return (rates, powers)


def summarize(inner_wide, signal_wide, log_rates):
    length, channels = inner_wide.shape
    block = min(16, length)
    blocks = length // block
    product = (inner_wide * signal_wide).reshape(blocks, block, channels)
    rates, powers = decay_tables(log_rates, block)
    tails = powers[:, ::-1, :]
    partial_sums = jnp.sum(product[:, None, :, :] * tails[None], axis=2)
    spans = jnp.arange(blocks - 1, -1, -1, dtype=jnp.float32) * block
    weights = jnp.exp(-rates[None] * spans[:, None, None])
    summary = jnp.sum(weights * partial_sums, axis=0)
    return (jnp.exp(-rates * length), summary, partial_sums)


def respond(outer_wide, inner_wide, signal_wide, residues, log_rates, partial_sums, incoming):
    length, channels = outer_wide.shape
    block = min(16, length)
    blocks = length // block
    product = (inner_wide * signal_wide).reshape(blocks, block, channels)
    rates, powers = decay_tables(log_rates, block)
    weights = residues * jnp.sqrt(2.0 * rates)
    taps = jnp.sum(weights[:, None, :] * powers, axis=0)
    local_part = taps[0][None, None, :] * product
    for lag in range(1, block):
        shifted = jnp.pad(product[:, : block - lag, :], ((0, 0), (lag, 0), (0, 0)))
        local_part = local_part + taps[lag][None, None, :] * shifted
    stride = jnp.exp(-rates * block)

    def advance(state, piece):
        return (stride * state + piece, state)

    _, starts = lax.scan(advance, incoming, partial_sums)
    heads = powers * jnp.exp(-rates)[:, None, :]
    carried = jnp.sum((starts * weights[None])[:, :, None, :] * heads[None], axis=1)
    return outer_wide * (local_part + carried).reshape(length, channels)


def per_device(outer_gate, inner_gate, signal, residues, log_rates, norm_gain, cotangent):
    length = outer_gate.shape[0]
    outer_wide = outer_gate.astype(jnp.float32)
    inner_wide = inner_gate.astype(jnp.float32)
    signal_wide = signal.astype(jnp.float32)
    (stride_all, summary, partial_sums), summary_back = jax.vjp(
        summarize, inner_wide, signal_wide, log_rates
    )
    identity = (jnp.ones_like(stride_all), jnp.zeros_like(summary))
    incoming = carried_in((stride_all, summary), ("ctx", "grp"), chain, identity, False)[1]
    mixed, respond_back = jax.vjp(
        respond, outer_wide, inner_wide, signal_wide, residues, log_rates, partial_sums, incoming
    )
    gain_wide = norm_gain.astype(jnp.float32)
    gained = cotangent.astype(jnp.float32) * gain_wide[None, :]
    squares, inner_products = lax.psum(
        (jnp.sum(mixed * mixed, axis=1), jnp.sum(gained * mixed, axis=1)), "tp"
    )
    scale = lax.rsqrt(squares / D + 1e-06)
    output = (mixed * scale[:, None] * gain_wide[None, :]).astype(jnp.bfloat16)
    grad_mixed = (
        scale[:, None] * gained - mixed * (scale * scale * scale * inner_products / D)[:, None]
    )
    grad_outer, inner_late, signal_late, residue_local, rate_late, sums_back, incoming_back = (
        respond_back(grad_mixed)
    )
    adjoint_state = carried_in((stride_all, incoming_back), ("ctx", "grp"), chain, identity, True)[
        1
    ]
    inner_early, signal_early, rate_early = summary_back(
        (adjoint_state * incoming, adjoint_state, sums_back)
    )
    residue_total, rate_total = lax.psum((residue_local, rate_late + rate_early), ("ctx", "grp"))
    factor = 1.0 / math.sqrt(length * lax.axis_size(("ctx", "grp")))
    return (
        output,
        grad_outer.astype(jnp.bfloat16),
        (inner_late + inner_early).astype(jnp.bfloat16),
        (signal_late + signal_early).astype(jnp.bfloat16),
        residue_total * factor,
        rate_total * factor,
    )


def solution(mesh):
    return jax.shard_map(
        per_device,
        mesh=mesh,
        in_specs=(
            P(("ctx", "grp"), "tp"),
            P(("ctx", "grp"), "tp"),
            P(("ctx", "grp"), "tp"),
            P(None, "tp"),
            P(None, "tp"),
            P("tp"),
            P(("ctx", "grp"), "tp"),
        ),
        out_specs=(
            P(("ctx", "grp"), "tp"),
            P(("ctx", "grp"), "tp"),
            P(("ctx", "grp"), "tp"),
            P(("ctx", "grp"), "tp"),
            P(None, "tp"),
            P(None, "tp"),
        ),
        check_vma=False,
    )
```

profile of v0, /device:TPU:8, one launch (start us, length us, event | category | flops | bytes accessed | tf_op | source)
XLA Modules:
  0.0 2042.7 jit_solution(14401418616088193679)
XLA Ops:
  7.2 1.6 fusion.23
  8.9 1.3 multiply_reduce_fusion.10
  10.2 3.8 rev.6
  14.0 1.1 convert_multiply_fusion.1
  15.1 2.0 multiply_reduce_fusion.5
  24.9 204.5 %all-gather.7.cloned.1.call-done = f32[1536,1024]{1,0:T(8,128)} async-done(((f32[16,1024]{1,0:T(8,128)}), f32[1536,1024]{1,0:T(8,128)}) %all-gather.7.cloned.1.call-update) | async-done | bytes 6291472 | tf_op jit(solution)/shard_map/all_gather | solution.py:15
  229.4 208.4 %all-gather.9.cloned.1.call-done = f32[1536,1024]{1,0:T(8,128)} async-done(((f32[16,1024]{1,0:T(8,128)}), f32[1536,1024]{1,0:T(8,128)}) %all-gather.9.cloned.1.call-update) | async-done | bytes 6291472 | tf_op jit(solution)/shard_map/all_gather | solution.py:15
  437.8 2.8 while.57
  437.8 0.9 bitcast_add_fusion.8
  438.8 0.9 bitcast_add_fusion.8
  440.7 7.3 while.58
  448.9 2.6 fusion.10
  453.0 14.2 all-reduce.47
  468.0 3.7 fusion.20
  471.7 2.4 multiply_reduce_fusion.1
  475.7 12.2 while.60
  488.6 1.3 slice_multiply_fusion.14
  489.9 1.3 slice_multiply_fusion.13
  491.2 1.3 slice_multiply_fusion.11
  492.6 1.4 slice_multiply_fusion.12
  493.9 1.4 slice_multiply_fusion.7
  495.3 1.4 slice_multiply_fusion.8
  496.7 1.4 slice_multiply_fusion.9
  498.1 1.4 slice_multiply_fusion.10
  499.6 1.6 slice_multiply_fusion
  506.4 267.8 %all-gather.11.cloned.1.call-done = f32[1536,1024]{1,0:T(8,128)} async-done(((f32[16,1024]{1,0:T(8,128)}), f32[1536,1024]{1,0:T(8,128)}) %all-gather.11.cloned.1.call-update) | async-done | bytes 6291472 | tf_op jit(solution)/shard_map/all_gather | solution.py:15
  774.2 85.3 %while.59 = (s32[]{:T(128)}, f32[16,1024]{1,0:T(8,128)S(1)}, s32[]{:T(128)}, f32[96,16,1024]{2,1,0:T(8,128)}, f32[96,16,1024]{2,1,0:T(8,128)}, /*index=5*/s32[]{:T(128)}, s32[]{:T(128)}, s32[]{:T(128)}, s32[]{:T(128)}) while((s32[]{:T(128)}, f32[16,1024]{1,0:T(8,128)S(1)}, s32[]{:T(128)}, f32[96,16,1024]{2,1,0:T(8,128)}, ...), condition=%wide.region_16.17_spmd, body=%wide.region_15.16_spmd.sunk | while | flops 32774 | bytes 262295 | solution.py:24
  776.1 0.9 bitcast_add_fusion.10
  777.9 0.9 bitcast_add_fusion.10
  779.8 0.9 bitcast_add_fusion.10
  781.6 0.9 bitcast_add_fusion.10
  783.5 0.9 bitcast_add_fusion.10
  785.3 0.9 bitcast_add_fusion.10
  787.2 0.9 bitcast_add_fusion.10
  789.0 0.9 bitcast_add_fusion.10
  791.8 0.9 bitcast_add_fusion.10
  793.6 0.9 bitcast_add_fusion.10
  795.5 0.9 bitcast_add_fusion.10
  797.3 0.9 bitcast_add_fusion.10
  799.2 0.9 bitcast_add_fusion.10
  801.0 0.9 bitcast_add_fusion.10
  802.9 0.9 bitcast_add_fusion.10
  804.8 0.9 bitcast_add_fusion.10
  806.6 0.9 bitcast_add_fusion.10
  809.4 0.9 bitcast_add_fusion.10
  811.2 0.9 bitcast_add_fusion.10
  813.1 0.9 bitcast_add_fusion.10
  814.9 0.9 bitcast_add_fusion.10
  816.8 0.9 bitcast_add_fusion.10
  818.6 0.9 bitcast_add_fusion.10
  820.5 0.9 bitcast_add_fusion.10
  822.3 0.9 bitcast_add_fusion.10
  824.2 0.9 bitcast_add_fusion.10
  827.0 0.9 bitcast_add_fusion.10
  859.6 1.9 multiply_reduce_fusion.11
  861.5 2.3 multiply_reduce_fusion
  863.8 3.3 add_add_fusion
  867.1 1.0 fusion.15
  868.1 3.8 rev.7
  872.8 1.9 multiply_reduce_fusion.8
  874.7 1.7 add_multiply_fusion
  876.4 1.6 fusion.21
  878.0 1156.6 %all-reduce.50.cloned.1.call-done = (f32[16,1024]{1,0:T(8,128)}, f32[16,1024]{1,0:T(8,128)}) async-done(((f32[16,1024]{1,0:T(8,128)}, f32[16,1024]{1,0:T(8,128)}), (f32[16,1024]{1,0:T(8,128)}, f32[16,1024]{1,0:T(8,128)})) %all-reduce.50.cloned.1.call-update) | async-done | bytes 131088 | tf_op jit(solution)/shard_map/psum | solution.py:107
  2034.6 1.5 broadcast_multiply_fusion.2
  (195 shorter events, 98.4 us)
Async XLA Ops:
  7.2 17.1 copy-start.27
  7.2 222.3 %all-gather.7.cloned.1.call-start = ((), (), s32[]{:S(2)}) async-start(), calls=%async_computation | async-start | bytes 6356992 | tf_op jit(solution)/shard_map/all_gather | solution.py:15
  8.8 15.4 copy-start.16
  8.8 429.0 %copy-start.19 = (f32[16,1024]{1,0:T(8,128)}, f32[16,1024]{1,0:T(8,128)S(1)}, u32[]{:S(2)}) copy-start(f32[16,1024]{1,0:T(8,128)S(1)} %get-tuple-element.443) | copy-start | bytes 196612
  8.8 429.0 %all-gather.9.cloned.1.call-start = ((), (), s32[]{:S(2)}) async-start(), calls=%async_computation.1 | async-start | bytes 6356992 | tf_op jit(solution)/shard_map/all_gather | solution.py:15
  14.0 426.6 %copy-start.28 = (f32[8]{0:T(128)}, f32[8]{0:T(128)S(1)}, u32[]{:S(2)}) copy-start(f32[8]{0:T(128)S(1)} %add_multiply_fusion.1) | copy-start | bytes 100
  17.1 0.8 copy-start.5
  18.7 755.5 %all-gather.11.cloned.1.call-start = ((), (), s32[]{:S(2)}) async-start(), calls=%async_computation.2 | async-start | bytes 6356992 | tf_op jit(solution)/shard_map/all_gather | solution.py:15
  447.9 20.0 copy-start.3
  447.9 4.3 copy-start.10
  448.0 4.3 copy-start.12
  448.0 20.0 copy-start.18
  448.0 0.8 copy-start.7
  451.4 0.8 copy-start
  467.2 4.5 copy-start.8
  467.9 3.7 copy-start.25
  467.9 3.8 copy-start.26
  468.0 6.1 copy-start.4
  474.1 27.0 %copy-start.22 = (f32[1,1024]{1,0:T(1,128)S(1)}, f32[1,1024]{1,0:T(1,128)}, u32[]{:S(2)}) copy-start(f32[1,1024]{1,0:T(1,128)} %get-tuple-element.435) | copy-start | bytes 12292
  474.1 27.9 %copy-start.21 = (f32[1,1024]{1,0:T(1,128)S(1)}, f32[1,1024]{1,0:T(1,128)}, u32[]{:S(2)}) copy-start(f32[1,1024]{1,0:T(1,128)} %get-tuple-element.434) | copy-start | bytes 12292
  474.1 28.8 %copy-start.20 = (f32[1,1024]{1,0:T(1,128)S(1)}, f32[1,1024]{1,0:T(1,128)}, u32[]{:S(2)}) copy-start(f32[1,1024]{1,0:T(1,128)} %get-tuple-element.433) | copy-start | bytes 12292
  487.9 0.6 copy-start.2
  487.9 371.7 %copy-start.6 = (f32[8,16,1024]{2,1,0:T(8,128)S(1)}, f32[8,16,1024]{2,1,0:T(8,128)}, u32[]{:S(2)}) copy-start(f32[8,16,1024]{2,1,0:T(8,128)} %get-tuple-element.700) | copy-start | bytes 1572868
  487.9 371.7 %copy-start.17 = (f32[16,1024]{1,0:T(8,128)S(1)}, f32[16,1024]{1,0:T(8,128)}, u32[]{:S(2)}) copy-start(f32[16,1024]{1,0:T(8,128)} %copy-done.16) | copy-start | bytes 196612
  488.5 1546.1 %all-reduce.50.cloned.1.call-start = ((), (), s32[]{:S(2)}) async-start(), calls=%async_computation.3 | async-start | bytes 262144 | tf_op jit(solution)/shard_map/psum | solution.py:107
  859.5 7.5 copy-start.14
  859.6 7.5 copy-start.15
  863.8 8.1 copy-start.23
  863.8 8.1 copy-start.24
  863.8 8.9 copy-start.9
  863.8 12.6 copy-start.1
  863.8 12.6 copy-start.11
  863.8 12.6 copy-start.13
Sparse Core Ops, SparseCore 0:
  14.1 215.2 all-gather.6
  235.5 202.2 all-gather.8
  488.7 285.4 all-gather.10
  876.5 1158.0 all-reduce.49
where the time goes:
time: 2050 us; the launch traced here: 2040 us
  waiting for transfers between devices  1840 us (90%)
  other arithmetic  157 us (8%)
    psum x1, waiting for transfers between devices, per_device(): lax.psum((residue_local, rate_late + rate_early), ('ctx', 'grp'))  1160 us
    all_gather x3, waiting for transfers between devices, carried_in(): gathered = jax.tree.map(lambda a: lax.all_gather(a, axis), part)  681 us
    add x95, other arithmetic, chain(): return (earlier[0] * later[0], earlier[1] * later[0] + later[1])  86 us
  transfers between devices with their start and end apart: 4, of which 4 were waited for; matrix products, arithmetic and copies ran while one was open for 2% of the time, Pallas kernels for 0%

commit v1 on v0

v1 whole, which is shorter than its diff:
```python
import math

import jax
import jax.numpy as jnp
from jax import lax
from jax.experimental import pallas as pl
from jax.experimental.pallas import tpu as pltpu
from jax.sharding import PartitionSpec as P

D = 8192
MODES = 16
ROWS = 8
LANES = 128
NX, NY = 4, 8
MESH = pl.DeviceIdType.MESH
F32 = jnp.float32
BF16 = jnp.bfloat16


def kernel(
    nz, nt, length, factor,
    outer_hbm, inner_hbm, signal_hbm, cot_hbm, residues_ref, log_rates_ref, gain_ref,
    output_ref, gouter_ref, ginner_ref, gsignal_ref, rgrad_ref, agrad_ref,
    outer_v, inner_v, signal_v, cot_v,
    tokens_p, tokens_r, tokens_w, mixed_n, sums_a, sums_b, cols_a, cols_b,
    rho_s, root_s, lam_s, wts_s, big_s,
    box_z, box_zd, box_zg,
    tot_s, totd_s, totg_s, pre_z, pre_zd, pre_zg,
    box_y, box_yd, box_yg, box_x, box_xd, box_xg, ret_s, retd_s, retg_s, box_r, box_rd, box_rg,
    xin_s, state_in, stated_in, adj_in,
    prm_s, prm_y, prm_x, prm_z, prm_g, box_t,
    in_sem, send_sem, recv_sem,
):
    ctx = lax.axis_index("ctx")
    x, y = ctx // NY, lax.rem(ctx, NY)
    z = lax.axis_index("grp")
    t = lax.axis_index("tp")
    block = float(length)

    def rows(start, size):
        return pl.ds(pl.multiple_of(start, size), size)

    places = {
        "z": (nz, z, lambda q: {"grp": q}),
        "y": (NY, y, lambda q: {"ctx": x * NY + q}),
        "x": (NX, x, lambda q: {"ctx": q * NY + y}),
        "t": (nt, t, lambda q: {"tp": q}),
    }
    used = [0]

    class Exchange:
        def __init__(self, axis, box, size, piece=None):
            self.n, self.me, self.device = places[axis]
            self.box, self.size = box, size
            self.piece = piece or (lambda q: self.slot(self.me))
            self.first = used[0]
            used[0] += self.n - 1

        def slot(self, q):
            return self.box.at[rows(q * self.size, self.size)]

        def copy(self, k, landing):
            peer = lax.rem(self.me + k, self.n)
            source = lax.rem(self.me + self.n - k, self.n)
            return pltpu.make_async_remote_copy(
                src_ref=self.piece(peer),
                dst_ref=self.slot(source if landing else self.me),
                send_sem=send_sem.at[self.first + k - 1],
                recv_sem=recv_sem.at[self.first + k - 1],
                device_id=self.device(peer),
                device_id_type=MESH,
            )

        def start(self):
            for k in range(1, self.n):
                self.copy(k, False).start()

        def wait(self):
            for k in range(1, self.n):
                self.copy(k, True).wait_recv()

        def drain(self):
            for k in range(1, self.n):
                self.copy(k, False).wait_send()

    span = MODES * ROWS
    own = 2 * ROWS
    mine = rows(y * own, own)

    def pick(ref):
        return lambda q: ref.at[rows(q * own, own)]

    gather_z = Exchange("z", box_z, span)
    gather_zd = Exchange("z", box_zd, span)
    gather_zg = Exchange("z", box_zg, span)
    split_y = Exchange("y", box_y, own, pick(tot_s))
    split_yd = Exchange("y", box_yd, own, pick(totd_s))
    split_yg = Exchange("y", box_yg, own, pick(totg_s))
    gather_x = Exchange("x", box_x, own)
    gather_xd = Exchange("x", box_xd, own)
    gather_xg = Exchange("x", box_xg, own)
    back_y = Exchange("y", box_r, own, pick(ret_s))
    back_yd = Exchange("y", box_rd, own, pick(retd_s))
    back_yg = Exchange("y", box_rg, own, pick(retg_s))
    norms = Exchange("t", box_t, ROWS)
    prm_split = Exchange("y", prm_y, 2 * own, lambda q: prm_s.at[rows(q * 2 * own, 2 * own)])
    prm_sum_x = Exchange("x", prm_x, 2 * own)
    prm_sum_z = Exchange("z", prm_z, 2 * own)
    prm_back = Exchange("y", prm_g, 2 * own)
    everything = [
        gather_z, gather_zd, gather_zg, split_y, split_yd, split_yg, gather_x, gather_xd, gather_xg,
        back_y, back_yd, back_yg, norms, prm_split, prm_sum_x, prm_sum_z, prm_back,
    ]

    loads = [
        pltpu.make_async_copy(src, dst, in_sem.at[i])
        for i, (src, dst) in enumerate(
            [(inner_hbm, inner_v), (signal_hbm, signal_v), (outer_hbm, outer_v), (cot_hbm, cot_v)]
        )
    ]
    for load in loads:
        load.start()

    barrier = pltpu.get_barrier_semaphore()
    partners = 0
    for axis in ("z", "y", "x", "t"):
        n, me, device = places[axis]
        for k in range(1, n):
            pl.semaphore_signal(
                barrier, inc=1, device_id=device(lax.rem(me + k, n)), device_id_type=MESH
            )
            partners += 1

    for half in range(MODES // 8):
        for j in range(ROWS):
            there = pl.ds(half * 64 + j, 8, stride=ROWS)
            lanes = slice(j * LANES, (j + 1) * LANES)
            rho = jnp.exp(log_rates_ref[half * 8 : half * 8 + 8, lanes])
            root = jnp.sqrt(2.0 * rho)
            rho_s[there, :] = rho
            root_s[there, :] = root
            wts_s[there, :] = residues_ref[half * 8 : half * 8 + 8, lanes] * root
    lam_s[...] = jnp.exp(-rho_s[...])
    big_s[...] = jnp.exp(-block * rho_s[...])

    def mode(ref, m, base=0):
        return ref[base + m * ROWS : base + (m + 1) * ROWS, :]

    def put(ref, m, value, base=0):
        ref[base + m * ROWS : base + (m + 1) * ROWS, :] = value

    def natural(body, step=16):
        def turn(i, carry):
            tokens = rows(i * step, step)
            for j in range(ROWS):
                body(tokens, j, slice(j * LANES, (j + 1) * LANES),
                     pl.ds(i * (step * ROWS) + j, step, stride=ROWS))
            return carry

        lax.fori_loop(0, length // step, turn, 0)

    def sweep(body, carry, unroll=8, reverse=False):
        def turn(i, carry):
            for u in range(unroll):
                at = i * unroll + u
                if reverse:
                    at = length - 1 - at
                carry = body(rows(at * ROWS, ROWS), carry)
            return carry

        return lax.fori_loop(0, length // unroll, turn, carry)

    zero = jnp.zeros((ROWS, LANES), F32)

    loads[0].wait()
    loads[1].wait()

    def multiply(tokens, j, lanes, place):
        tokens_p[place, :] = inner_v[tokens, lanes].astype(F32) * signal_v[tokens, lanes].astype(F32)

    natural(multiply)

    decay = [mode(lam_s, m) for m in range(MODES)]

    def leave(at, state):
        p = tokens_p[at, :]
        return tuple(d * s + p for d, s in zip(decay, state))

    state = sweep(leave, (zero,) * MODES)
    for m in range(MODES):
        box_z[rows(z * span + m * ROWS, ROWS), :] = state[m]

    pl.semaphore_wait(barrier, partners)
    gather_z.start()

    for half in range(2):
        some = range(half * 8, half * 8 + 8)
        decay = [mode(lam_s, m) for m in some]
        weight = [mode(wts_s, m) for m in some]

        def respond(at, carry, decay=decay, weight=weight, half=half):
            p = tokens_p[at, :]
            lagged = [d * (a + s) for d, a, s in zip(decay, carry[8:], carry[:8])]
            state = [d * s + p for d, s in zip(decay, carry[:8])]
            terms = [w * s for w, s in zip(weight, state)]
            while len(terms) > 1:
                terms = [a + b for a, b in zip(terms[::2], terms[1::2])]
            tokens_r[at, :] = terms[0] if half == 0 else tokens_r[at, :] + terms[0]
            return tuple(state + lagged)

        carry = sweep(respond, (zero,) * 16)
        for i, m in enumerate(some):
            box_zd[rows(z * span + m * ROWS, ROWS), :] = carry[8 + i]
    gather_zd.start()

    rho_own = rho_s[mine, :]
    step_y = jnp.exp((-nz * block) * rho_own)
    step_x = jnp.exp((-nz * NY * block) * rho_own)

    def total_z(box, total, pre, forward):
        order = range(nz) if forward else range(nz - 1, -1, -1)
        for m in range(MODES):
            hop = mode(big_s, m)
            running, chosen = zero, zero
            for q in order:
                chosen = jnp.where(z == q, running, chosen)
                running = hop * running + mode(box, m, q * span)
            put(total, m, running)
            put(pre, m, chosen)

    def prefix_y(box, pre, box_next, forward):
        order = range(NY) if forward else range(NY - 1, -1, -1)
        running = jnp.zeros((own, LANES), F32)
        for q in order:
            pre[q * own : (q + 1) * own, :] = running
            running = step_y * running + box[q * own : (q + 1) * own, :]
        box_next[rows(x * own, own), :] = running

    def return_y(box, pre, forward):
        order = range(NX) if forward else range(NX - 1, -1, -1)
        came = jnp.zeros((own, LANES), F32)
        for q in order:
            earlier = (q < x) if forward else (q > x)
            came = jnp.where(earlier, step_x * came + box[q * own : (q + 1) * own, :], came)
        xin_s[...] = came
        for q in (range(NY) if forward else range(NY - 1, -1, -1)):
            pre[q * own : (q + 1) * own, :] = pre[q * own : (q + 1) * own, :] + came
            came = step_y * came

    def keep_own(box, source):
        box[mine, :] = source[mine, :]

    def power_z(m, count):
        hop = mode(big_s, m)
        power, chosen = jnp.ones_like(hop), jnp.ones_like(hop)
        for q in range(1, nz):
            power = power * hop
            chosen = jnp.where(count == q, power, chosen)
        return chosen

    gather_z.wait()
    total_z(box_z, tot_s, pre_z, True)
    split_y.start()
    keep_own(box_y, tot_s)
    split_y.wait()
    prefix_y(box_y, ret_s, box_x, True)
    gather_x.start()
    gather_x.wait()
    return_y(box_x, ret_s, True)
    back_y.start()
    keep_own(box_r, ret_s)

    gather_zd.wait()
    for m in range(MODES):
        hop = mode(big_s, m)
        run, rund, chosen = zero, zero, zero
        for q in range(nz):
            chosen = jnp.where(z == q, rund, chosen)
            rund = hop * (rund + block * run) + mode(box_zd, m, q * span)
            run = hop * run + mode(box_z, m, q * span)
        put(totd_s, m, rund)
        put(pre_zd, m, chosen)
    split_yd.start()
    keep_own(box_yd, totd_s)

    loads[2].wait()
    loads[3].wait()
    back_y.wait()
    for m in range(MODES):
        put(state_in, m, mode(pre_z, m) + power_z(m, z) * mode(box_r, m))

    decay = [mode(lam_s, m) for m in range(MODES)]
    fade = tuple(mode(wts_s, m) * mode(state_in, m) for m in range(MODES))

    def carried(at, fade):
        fade = tuple(d * f for d, f in zip(decay, fade))
        terms = list(fade)
        while len(terms) > 1:
            terms = [a + b for a, b in zip(terms[::2], terms[1::2])]
        tokens_r[at, :] = tokens_r[at, :] + terms[0]
        return fade

    sweep(carried, fade)

    def mix(i, carry):
        tokens = rows(i * 16, 16)
        squares = jnp.zeros((16, LANES), F32)
        inners = jnp.zeros((16, LANES), F32)
        for j in range(ROWS):
            lanes = slice(j * LANES, (j + 1) * LANES)
            mixed = outer_v[tokens, lanes].astype(F32) * tokens_r[pl.ds(i * 128 + j, 16, stride=ROWS), :]
            gained = cot_v[tokens, lanes].astype(F32) * gain_ref[:, lanes]
            mixed_n[tokens, lanes] = mixed
            squares = squares + mixed * mixed
            inners = inners + gained * mixed
        sums_a[tokens, :] = squares
        sums_b[tokens, :] = inners
        return carry

    lax.fori_loop(0, length // 16, mix, 0)

    def across(a, b):
        return lax.dot_general(
            a, b, (((1,), (1,)), ((), ())), precision=lax.Precision.HIGHEST,
            preferred_element_type=F32,
        )

    ones = jnp.ones((ROWS, LANES), F32)
    upper = lax.broadcasted_iota(jnp.int32, (ROWS, length), 0) < 4
    box_t[rows(t * ROWS, ROWS), :] = jnp.where(
        upper, across(ones, sums_a[...]), across(ones, sums_b[...])
    )
    norms.start()

    split_yd.wait()
    run = jnp.zeros((own, LANES), F32)
    rund = run
    for q in range(NY):
        retd_s[q * own : (q + 1) * own, :] = rund
        rund = step_y * (rund + (nz * block) * run) + box_yd[q * own : (q + 1) * own, :]
        run = step_y * run + box_y[q * own : (q + 1) * own, :]
    box_xd[rows(x * own, own), :] = rund
    gather_xd.start()

    norms.wait()
    both = jnp.zeros((ROWS, length), F32)
    for q in range(nt):
        both = both + box_t[q * ROWS : (q + 1) * ROWS, :]
    scale = lax.rsqrt(both[0:1, :] / D + 1e-06)
    pull = scale * scale * scale * both[4:5, :] / D
    row_id = lax.broadcasted_iota(jnp.int32, (length, length), 0)
    col_id = lax.broadcasted_iota(jnp.int32, (length, length), 1)
    square = jnp.ones((LANES, length), F32)
    cols_a[...] = across(jnp.where(row_id == col_id, scale, 0.0), square)
    cols_b[...] = across(jnp.where(row_id == col_id, pull, 0.0), square)

    def finish(i, carry):
        tokens = rows(i * 16, 16)
        a, b = cols_a[tokens, :], cols_b[tokens, :]
        for j in range(ROWS):
            lanes = slice(j * LANES, (j + 1) * LANES)
            place = pl.ds(i * 128 + j, 16, stride=ROWS)
            mixed = mixed_n[tokens, lanes]
            gain = gain_ref[:, lanes]
            gained = cot_v[tokens, lanes].astype(F32) * gain
            grad = a * gained - mixed * b
            tokens_w[place, :] = grad * outer_v[tokens, lanes].astype(F32)
            output_ref[tokens, lanes] = (mixed * a * gain).astype(BF16)
            gouter_ref[tokens, lanes] = (grad * tokens_r[place, :]).astype(BF16)
        return carry

    lax.fori_loop(0, length // 16, finish, 0)

    def leave_back(at, adjoint):
        w = tokens_w[at, :]
        return tuple(d * a + w for d, a in zip(decay, adjoint))

    adjoint = sweep(leave_back, (zero,) * MODES, reverse=True)
    for m in range(MODES):
        box_zg[rows(z * span + m * ROWS, ROWS), :] = decay[m] * adjoint[m]
    gather_zg.start()

    gather_xd.wait()
    came = jnp.zeros((own, LANES), F32)
    camed = came
    for q in range(NX):
        camed = jnp.where(
            q < x,
            step_x * (camed + (nz * NY * block) * came) + box_xd[q * own : (q + 1) * own, :],
            camed,
        )
        came = jnp.where(q < x, step_x * came + box_x[q * own : (q + 1) * own, :], came)
    for q in range(NY):
        retd_s[q * own : (q + 1) * own, :] = retd_s[q * own : (q + 1) * own, :] + camed
        camed = step_y * (camed + (nz * block) * came)
        came = step_y * came
    back_yd.start()
    keep_own(box_rd, retd_s)

    for half in range(2):
        some = range(half * 8, half * 8 + 8)
        decay8 = [mode(lam_s, m) for m in some]
        weight8 = [mode(wts_s, m) for m in some]

        def pull_back(at, adjoint, decay=decay8, weight=weight8, half=half):
            w = tokens_w[at, :]
            adjoint = tuple(d * a + w for d, a in zip(decay, adjoint))
            terms = [k * a for k, a in zip(weight, adjoint)]
            while len(terms) > 1:
                terms = [a + b for a, b in zip(terms[::2], terms[1::2])]
            mixed_rows[at, :] = terms[0] if half == 0 else mixed_rows[at, :] + terms[0]
            return adjoint

        mixed_rows = tokens_r
        sweep(pull_back, (zero,) * 8, reverse=True)

    back_yd.wait()
    zf = z.astype(F32)
    for m in range(MODES):
        start_d = mode(box_rd, m) + (block * zf) * mode(box_r, m)
        put(stated_in, m, mode(pre_zd, m) + power_z(m, z) * start_d)

    for half in range(2):
        some = range(half * 8, half * 8 + 8)
        decay8 = [mode(lam_s, m) for m in some]

        def correlate(at, carry, decay=decay8):
            p, w = tokens_p[at, :], tokens_w[at, :]
            state, lagged, first, second = carry[:8], carry[8:16], carry[16:24], carry[24:]
            lagged = [d * (a + s) for d, a, s in zip(decay, lagged, state)]
            state = [d * s + p for d, s in zip(decay, state)]
            first = [f + w * s for f, s in zip(first, state)]
            second = [f + w * a for f, a in zip(second, lagged)]
            return tuple(state + lagged + first + second)

        carry = sweep(
            correlate,
            tuple(mode(state_in, m) for m in some)
            + tuple(mode(stated_in, m) for m in some)
            + (zero,) * 16,
            unroll=4,
        )
        for i, m in enumerate(some):
            base = (m // 2) * 2 * own + (m % 2) * ROWS
            prm_s[base : base + ROWS, :] = carry[16 + i]
            prm_s[base + own : base + own + ROWS, :] = carry[24 + i]
    prm_split.start()
    prm_y[rows(y * 2 * own, 2 * own), :] = prm_s[rows(y * 2 * own, 2 * own), :]

    def add_up(box, n):
        total = box[0 : 2 * own, :]
        for q in range(1, n):
            total = total + box[q * 2 * own : (q + 1) * 2 * own, :]
        return total

    gather_zg.wait()
    total_z(box_zg, totg_s, pre_zg, False)
    split_yg.start()
    keep_own(box_yg, totg_s)
    prm_split.wait()
    prm_x[rows(x * 2 * own, 2 * own), :] = add_up(prm_y, NY)
    prm_sum_x.start()
    split_yg.wait()
    prefix_y(box_yg, retg_s, box_xg, False)
    gather_xg.start()
    prm_sum_x.wait()
    prm_z[rows(z * 2 * own, 2 * own), :] = add_up(prm_x, NX)
    prm_sum_z.start()
    gather_xg.wait()
    return_y(box_xg, retg_s, False)
    back_yg.start()
    keep_own(box_rg, retg_s)
    prm_sum_z.wait()
    prm_g[rows(y * 2 * own, 2 * own), :] = add_up(prm_z, nz)
    prm_back.start()

    back_yg.wait()
    for m in range(MODES):
        put(adj_in, m, mode(pre_zg, m) + power_z(m, nz - 1 - z) * mode(box_rg, m))
    fade = tuple(mode(wts_s, m) * mode(adj_in, m) for m in range(MODES))

    def carried_back(at, fade):
        terms = list(fade)
        while len(terms) > 1:
            terms = [a + b for a, b in zip(terms[::2], terms[1::2])]
        tokens_r[at, :] = tokens_r[at, :] + terms[0]
        return tuple(d * f for d, f in zip(decay, fade))

    sweep(carried_back, fade, reverse=True)

    def last(tokens, j, lanes, place):
        grad = tokens_r[place, :]
        ginner_ref[tokens, lanes] = (grad * signal_v[tokens, lanes].astype(F32)).astype(BF16)
        gsignal_ref[tokens, lanes] = (grad * inner_v[tokens, lanes].astype(F32)).astype(BF16)

    natural(last)

    prm_back.wait()
    prm_split.drain()
    for m in range(MODES):
        base = (m // 2) * 2 * own + (m % 2) * ROWS
        first = prm_g[base : base + ROWS, :]
        second = prm_g[base + own : base + own + ROWS, :]
        put(prm_s, m, factor * (mode(root_s, m) * first))
        put(prm_s, m, factor * (mode(wts_s, m) * (0.5 * first - mode(rho_s, m) * second)), span)
    for half in range(MODES // 8):
        for j in range(ROWS):
            lanes = slice(j * LANES, (j + 1) * LANES)
            rgrad_ref[half * 8 : half * 8 + 8, lanes] = prm_s[pl.ds(half * 64 + j, 8, stride=ROWS), :]
            agrad_ref[half * 8 : half * 8 + 8, lanes] = prm_s[
                pl.ds(span + half * 64 + j, 8, stride=ROWS), :
            ]
    for exchange in everything:
        if exchange is not prm_split:
            exchange.drain()


def solution(mesh):
    nz, nt = mesh.shape["grp"], mesh.shape["tp"]
    blocks = mesh.shape["ctx"] * nz
    assert mesh.shape["ctx"] == NX * NY

    def step(outer_gate, inner_gate, signal, residues, log_rates, norm_gain, cotangent):
        length, channels = outer_gate.shape
        assert channels == ROWS * LANES and length == LANES and residues.shape[0] == MODES
        factor = 1.0 / math.sqrt(length * blocks)
        span, own = MODES * ROWS, 2 * ROWS

        def f32(count):
            return pltpu.VMEM((count, LANES), F32)

        wide = pltpu.VMEM((length, channels), BF16)
        exchanges = 4 * (nz - 1) + 8 * (NY - 1) + 4 * (NX - 1) + (nt - 1)
        scratch = (
            [wide] * 4
            + [f32(length * ROWS)] * 3
            + [pltpu.VMEM((length, channels), F32)]
            + [f32(length)] * 4
            + [f32(span)] * 5
            + [f32(nz * span)] * 3
            + [f32(span)] * 6
            + [f32(NY * own)] * 3
            + [f32(NX * own)] * 3
            + [f32(NY * own)] * 6
            + [f32(own)]
            + [f32(span)] * 3
            + [f32(2 * span), f32(2 * NY * own), f32(2 * NX * own), f32(2 * nz * own), f32(2 * NY * own)]
            + [f32(nt * ROWS)]
            + [
                pltpu.SemaphoreType.DMA((4,)),
                pltpu.SemaphoreType.DMA((exchanges,)),
                pltpu.SemaphoreType.DMA((exchanges,)),
            ]
        )
        vmem = pl.BlockSpec(memory_space=pltpu.VMEM)
        hbm = pl.BlockSpec(memory_space=pl.ANY)
        tokens = jax.ShapeDtypeStruct((length, channels), BF16)
        params = jax.ShapeDtypeStruct(residues.shape, F32)

        def body(*refs):
            kernel(nz, nt, length, factor, *refs)

        return pl.pallas_call(
            body,
            out_shape=(tokens,) * 4 + (params,) * 2,
            in_specs=[hbm] * 4 + [vmem] * 3,
            out_specs=(vmem,) * 6,
            scratch_shapes=scratch,
            compiler_params=pltpu.CompilerParams(
                collective_id=0, has_side_effects=True, vmem_limit_bytes=40 * 1024 * 1024
            ),
            name="hyena",
        )(
            outer_gate, inner_gate, signal, cotangent, residues, log_rates,
            norm_gain.astype(F32)[None, :],
        )

    wide, narrow = P(("ctx", "grp"), "tp"), P(None, "tp")
    return jax.shard_map(
        step,
        mesh=mesh,
        in_specs=(wide, wide, wide, narrow, narrow, P("tp"), wide),
        out_specs=(wide,) * 4 + (narrow,) * 2,
        check_vma=False,
    )
```

time: 2050 us -> 92.4 us (0.05)
  the two profiles are of different devices: /device:TPU:8 before, /device:TPU:4 now
where the time goes in v1:
time: 92.4 us; the launch traced here: 92.1 us
  Pallas kernels  81.2 us (88%)
  local copies, waits for them, and re-layouts  9.55 us (10%)
    pallas_call x1, Pallas kernels, step(): pl.pallas_call(body, out_shape=(tokens,) * 4 + (params,) * 2, in_specs=[h...  81.2 us
    unnamed x18, local copies, waits for them, and re-layouts  9.55 us

profile of v1, /device:TPU:4, one launch (start us, length us, event | category | flops | bytes accessed | tf_op | source)
XLA Modules:
  0.0 92.1 jit_solution(17413077108731854699)
XLA Ops:
  0.6 0.7 broadcast_in_dim.7
  1.3 0.0 copy-start
  1.3 0.9 %copy-done = bf16[128,1024]{1,0:T(8,128)(2,1)S(1)} copy-done((bf16[128,1024]{1,0:T(8,128)(2,1)S(1)}, bf16[128,1024]{1,0:T(8,128)(2,1)}, u32[]{:S(2)}) %copy-start) | copy-done | bytes 262168
  2.3 0.0 copy-start.1
  2.3 0.9 %copy-done.1 = bf16[128,1024]{1,0:T(8,128)(2,1)S(1)} copy-done((bf16[128,1024]{1,0:T(8,128)(2,1)S(1)}, bf16[128,1024]{1,0:T(8,128)(2,1)}, u32[]{:S(2)}) %copy-start.1) | copy-done | bytes 262168
  3.2 0.0 copy-start.2
  3.2 0.9 %copy-done.2 = bf16[128,1024]{1,0:T(8,128)(2,1)S(1)} copy-done((bf16[128,1024]{1,0:T(8,128)(2,1)S(1)}, bf16[128,1024]{1,0:T(8,128)(2,1)}, u32[]{:S(2)}) %copy-start.2) | copy-done | bytes 262168
  4.2 0.0 copy-start.3
  4.2 0.9 %copy-done.3 = bf16[128,1024]{1,0:T(8,128)(2,1)S(1)} copy-done((bf16[128,1024]{1,0:T(8,128)(2,1)S(1)}, bf16[128,1024]{1,0:T(8,128)(2,1)}, u32[]{:S(2)}) %copy-start.3) | copy-done | bytes 262168
  5.1 0.0 copy-start.4
  5.1 0.8 copy-done.4
  6.0 0.0 copy-start.5
  6.0 0.8 copy-done.5
  6.8 81.2 %hyena.1 = (bf16[128,1024]{1,0:T(8,128)(2,1)S(1)}, bf16[128,1024]{1,0:T(8,128)(2,1)S(1)}, bf16[128,1024]{1,0:T(8,128)(2,1)S(1)}, bf16[128,1024]{1,0:T(8,128)(2,1...) custom-call(bf16[128,1024]{1,0:T(8,128)(2,1)S(1)} %copy-done, bf16[128,1024]{1,0:T(8,128)(2,1)S(1)} %copy-done.1, ...), custom_call_target="tpu_custom_call" | custom-call | tf_op jit(solution)/shard_map/hyena/pallas_call | solution.py:563
  88.0 0.7 copy.19
  88.7 0.7 copy.20
  89.4 0.7 copy.21
  90.1 0.7 copy.22
  90.8 0.6 copy.23
  91.4 0.6 copy.24
Async XLA Ops:
  1.3 0.9 %copy-start = (bf16[128,1024]{1,0:T(8,128)(2,1)S(1)}, bf16[128,1024]{1,0:T(8,128)(2,1)}, u32[]{:S(2)}) copy-start(bf16[128,1024]{1,0:T(8,128)(2,1)} %refs_0_.1) | copy-start | bytes 786436
  2.3 0.9 %copy-start.1 = (bf16[128,1024]{1,0:T(8,128)(2,1)S(1)}, bf16[128,1024]{1,0:T(8,128)(2,1)}, u32[]{:S(2)}) copy-start(bf16[128,1024]{1,0:T(8,128)(2,1)} %refs_1_.1) | copy-start | bytes 786436
  3.2 0.9 %copy-start.2 = (bf16[128,1024]{1,0:T(8,128)(2,1)S(1)}, bf16[128,1024]{1,0:T(8,128)(2,1)}, u32[]{:S(2)}) copy-start(bf16[128,1024]{1,0:T(8,128)(2,1)} %refs_2_.1) | copy-start | bytes 786436
  4.2 0.9 %copy-start.3 = (bf16[128,1024]{1,0:T(8,128)(2,1)S(1)}, bf16[128,1024]{1,0:T(8,128)(2,1)}, u32[]{:S(2)}) copy-start(bf16[128,1024]{1,0:T(8,128)(2,1)} %refs_3_.1) | copy-start | bytes 786436
  5.1 0.8 copy-start.4
  6.0 0.8 copy-start.5

commit v2 on v1

v2 whole, which is shorter than its diff:
```python
import math

import jax
import jax.numpy as jnp
from jax import lax
from jax.experimental import pallas as pl
from jax.experimental.pallas import tpu as pltpu
from jax.sharding import PartitionSpec as P

D = 8192
MODES = 16
ROWS = 8
LANES = 128
NX, NY = 4, 8
MESH = pl.DeviceIdType.MESH
F32 = jnp.float32
BF16 = jnp.bfloat16
HALF = MODES // 2
FLOWS = ("s_first", "s_last", "d_first", "d_last", "g_first", "g_last")


def layout(nz, nt, length):
    span, own = HALF * ROWS, ROWS
    shapes = {"tokens_p": length * ROWS, "tokens_r": length * ROWS, "tokens_w": length * ROWS}
    for name in ("sums_a", "sums_b", "cols_a", "cols_b"):
        shapes[name] = length
    for name in ("rho_s", "root_s", "lam_s", "wts_s", "big_s", "state_in", "stated_in", "adj_in"):
        shapes[name] = MODES * ROWS
    for flow in FLOWS:
        shapes |= {
            flow + ".loc": span, flow + ".out": nz * span, flow + ".box_z": nz * span,
            flow + ".tot": span, flow + ".pre": span, flow + ".box_y": NY * own,
            flow + ".box_x": NX * own, flow + ".ret": NY * own, flow + ".box_r": NY * own,
        }
    pair = 4 * ROWS
    shapes |= {
        "prm_s": NY * pair, "prm_y": NY * pair, "prm_x": NX * pair, "prm_z": nz * pair,
        "prm_g": NY * pair, "fin_s": 2 * MODES * ROWS, "box_t": nt * ROWS,
    }
    return shapes


def kernel(
    nz, nt, length, factor,
    outer_hbm, inner_hbm, signal_hbm, cot_hbm, residues_hbm, log_rates_hbm, gain_hbm,
    output_ref, gouter_ref, ginner_ref, gsignal_ref, rgrad_ref, agrad_ref,
    outer_v, inner_v, signal_v, cot_v, residues_v, log_rates_v, gain_v, gain_ref, mixed_n,
    in_sem, send_sem, recv_sem, *scratch,
):
    at = dict(zip(layout(nz, nt, length), scratch))
    tokens_p, tokens_r, tokens_w = at["tokens_p"], at["tokens_r"], at["tokens_w"]
    rho_s, root_s, lam_s, wts_s, big_s = (at[k] for k in ("rho_s", "root_s", "lam_s", "wts_s", "big_s"))
    prm_s, prm_y, prm_x, prm_z, prm_g = (at[k] for k in ("prm_s", "prm_y", "prm_x", "prm_z", "prm_g"))
    box_t, fin_s = at["box_t"], at["fin_s"]

    ctx = lax.axis_index("ctx")
    x, y = ctx // NY, lax.rem(ctx, NY)
    z = lax.axis_index("grp")
    t = lax.axis_index("tp")
    block = float(length)

    def rows(start, size):
        return pl.ds(pl.multiple_of(start, size), size)

    places = {
        "z": (nz, z, lambda q: {"grp": q}),
        "y": (NY, y, lambda q: {"ctx": x * NY + q}),
        "x": (NX, x, lambda q: {"ctx": q * NY + y}),
        "t": (nt, t, lambda q: {"tp": q}),
    }
    used = [0]
    everything = []

    class Exchange:
        def __init__(self, axis, box, size, piece=None):
            self.n, self.me, self.device = places[axis]
            self.box, self.size = box, size
            self.piece = piece or (lambda q: self.slot(self.me))
            self.first = used[0]
            used[0] += self.n - 1
            self.far_first = sorted(range(1, self.n), key=lambda k: -min(k, self.n - k))
            everything.append(self)

        def slot(self, q):
            return self.box.at[rows(q * self.size, self.size)]

        def copy(self, k, landing):
            peer = lax.rem(self.me + k, self.n)
            source = lax.rem(self.me + self.n - k, self.n)
            return pltpu.make_async_remote_copy(
                src_ref=self.piece(peer),
                dst_ref=self.slot(source if landing else self.me),
                send_sem=send_sem.at[self.first + k - 1],
                recv_sem=recv_sem.at[self.first + k - 1],
                device_id=self.device(peer),
                device_id_type=MESH,
            )

        def start(self):
            for k in self.far_first:
                self.copy(k, False).start()

        def wait(self):
            for k in range(1, self.n):
                self.copy(k, True).wait_recv()

        def drain(self):
            for k in range(1, self.n):
                self.copy(k, False).wait_send()

    span, own = HALF * ROWS, ROWS
    mine = rows(y * own, own)
    zero = jnp.zeros((ROWS, LANES), F32)

    def mode(ref, m, base=0):
        return ref[base + m * ROWS : base + (m + 1) * ROWS, :]

    def put(ref, m, value, base=0):
        ref[base + m * ROWS : base + (m + 1) * ROWS, :] = value

    def advance(value, low, power, count):
        return power * value if low is None else power * (value + (block * count) * low)

    class Flow:
        def __init__(self, name, first, forward, low=None):
            self.first, self.low = first, low
            self.m0 = 0 if first else HALF
            for key in ("loc", "out", "box_z", "tot", "pre", "box_y", "box_x", "ret", "box_r"):
                setattr(self, key, at[name + "." + key])
            self.zi = z if forward else nz - 1 - z
            self.order = lambda n: range(n) if forward else range(n - 1, -1, -1)
            self.place = lambda q: q if forward else nz - 1 - q
            self.before = (lambda q: q < x) if forward else (lambda q: q > x)
            self.ex_z = Exchange(
                "z", self.box_z, span, None if first else lambda q: self.out.at[rows(q * span, span)]
            )
            self.ex_y = Exchange("y", self.box_y, own, lambda q: self.tot.at[rows(q * own, own)])
            self.ex_x = Exchange("x", self.box_x, own)
            self.ex_r = Exchange("y", self.box_r, own, lambda q: self.ret.at[rows(q * own, own)])

        def hop(self, m):
            return mode(big_s, self.m0 + m)

        def power(self, m, count):
            hop = self.hop(m)
            power, chosen = jnp.ones_like(hop), jnp.ones_like(hop)
            for q in range(1, nz):
                power = power * hop
                chosen = jnp.where(count == q, power, chosen)
            return chosen

        def lower(self, ref_name, start, dynamic=False):
            if self.low is None:
                return None
            ref = getattr(self.low, ref_name)
            return ref[rows(start, ROWS), :] if dynamic else ref[start : start + ROWS, :]

        def begin(self, values):
            if self.first:
                for m in range(HALF):
                    self.box_z[rows(z * span + m * ROWS, ROWS), :] = values[m]
                return
            count = nz - 1 - self.zi
            for m in range(HALF):
                put(self.loc, m, values[m])
                put(self.tot, m, advance(
                    values[m], self.lower("loc", m * ROWS), self.power(m, count), count.astype(F32)))

        def send(self):
            if self.first:
                self.ex_z.start()
            else:
                self.send_y()

        def send_y(self):
            self.ex_y.start()
            self.box_y[mine, :] = self.tot[mine, :]

        def total(self):
            self.ex_z.wait()
            for m in range(HALF):
                hop = self.hop(m)
                running, lower, chosen = zero, zero, zero
                for q in self.order(nz):
                    chosen = jnp.where(z == q, running, chosen)
                    came = mode(self.box_z, m, q * span)
                    if self.low is None:
                        running = hop * running + came
                    else:
                        running = hop * (running + block * lower) + came
                        lower = hop * lower + mode(self.low.box_z, m, q * span)
                put(self.tot, m, running)
                put(self.pre, m, chosen)
            self.send_y()

        def steps(self):
            rho = rho_s[rows((self.m0 + y) * ROWS, ROWS), :]
            return jnp.exp((-nz * block) * rho), jnp.exp((-nz * NY * block) * rho)

        def prefix(self):
            self.ex_y.wait()
            step_y, _ = self.steps()
            running, lower = zero, (None if self.low is None else zero)
            for q in self.order(NY):
                put(self.ret, q, running)
                running = advance(running, lower, step_y, nz) + mode(self.box_y, q)
                if self.low is not None:
                    lower = step_y * lower + mode(self.low.box_y, q)
            self.box_x[rows(x * own, own), :] = running
            self.ex_x.start()

        def give_back(self):
            self.ex_x.wait()
            step_y, step_x = self.steps()
            came, lower = zero, (None if self.low is None else zero)
            for q in self.order(NX):
                earlier = self.before(q)
                came = jnp.where(earlier, advance(came, lower, step_x, nz * NY) + mode(self.box_x, q), came)
                if self.low is not None:
                    lower = jnp.where(earlier, step_x * lower + mode(self.low.box_x, q), lower)
            for q in self.order(NY):
                put(self.ret, q, mode(self.ret, q) + came)
                came = advance(came, lower, step_y, nz)
                if self.low is not None:
                    lower = step_y * lower
            self.ex_r.start()
            self.box_r[mine, :] = self.ret[mine, :]

        def last_z(self):
            self.ex_r.wait()
            for m in range(HALF):
                start, loc = mode(self.box_r, m), mode(self.loc, m)
                start_low, loc_low = self.lower("box_r", m * ROWS), self.lower("loc", m * ROWS)
                hop = self.hop(m)
                power = jnp.ones_like(hop)
                for qi in range(nz):
                    value = advance(start, start_low, power, qi)
                    if qi > 0:
                        count = qi - 1 - self.zi
                        near = advance(loc, loc_low, self.power(m, count), count.astype(F32))
                        value = value + jnp.where(self.zi < qi, near, 0.0)
                    put(self.out, m, value, self.place(qi) * span)
                    power = power * hop
            self.ex_z.start()
            here = rows(z * span, span)
            self.box_z[here, :] = self.out[here, :]

        def arrived(self):
            if self.first:
                self.ex_r.wait()
                return [
                    mode(self.pre, m) + advance(
                        mode(self.box_r, m), self.lower("box_r", m * ROWS),
                        self.power(m, self.zi), self.zi.astype(F32))
                    for m in range(HALF)
                ]
            self.ex_z.wait()
            return [sum(mode(self.box_z, m, q * span) for q in range(1, nz)) + mode(self.box_z, m)
                    for m in range(HALF)]

    sa, sb = Flow("s_first", True, True), Flow("s_last", False, True)
    da, db = Flow("d_first", True, True, sa), Flow("d_last", False, True, sb)
    ga, gb = Flow("g_first", True, False), Flow("g_last", False, False)
    pair = 4 * ROWS
    norms = Exchange("t", box_t, ROWS)
    prm_split = Exchange("y", prm_y, pair, lambda q: prm_s.at[rows(q * pair, pair)])
    prm_sum_x = Exchange("x", prm_x, pair)
    prm_sum_z = Exchange("z", prm_z, pair)
    prm_back = Exchange("y", prm_g, pair)

    loads = [
        pltpu.make_async_copy(src, dst, in_sem.at[i])
        for i, (src, dst) in enumerate([
            (log_rates_hbm, log_rates_v), (residues_hbm, residues_v), (inner_hbm, inner_v),
            (signal_hbm, signal_v), (outer_hbm, outer_v), (cot_hbm, cot_v), (gain_hbm, gain_v),
        ])
    ]
    for load in loads:
        load.start()

    barrier = pltpu.get_barrier_semaphore()
    partners = 0
    for axis in ("z", "y", "x", "t"):
        n, me, device = places[axis]
        for k in range(1, n):
            pl.semaphore_signal(
                barrier, inc=1, device_id=device(lax.rem(me + k, n)), device_id_type=MESH
            )
            partners += 1

    loads[0].wait()
    loads[1].wait()
    for half in range(MODES // 8):
        for j in range(ROWS):
            there = pl.ds(half * 64 + j, 8, stride=ROWS)
            lanes = slice(j * LANES, (j + 1) * LANES)
            rho = jnp.exp(log_rates_v[half * 8 : half * 8 + 8, lanes])
            root = jnp.sqrt(2.0 * rho)
            rho_s[there, :] = rho
            root_s[there, :] = root
            wts_s[there, :] = residues_v[half * 8 : half * 8 + 8, lanes] * root
    lam_s[...] = jnp.exp(-rho_s[...])
    big_s[...] = jnp.exp(-block * rho_s[...])

    def natural(body, step=16):
        def turn(i, carry):
            tokens = rows(i * step, step)
            for j in range(ROWS):
                body(tokens, slice(j * LANES, (j + 1) * LANES),
                     pl.ds(i * (step * ROWS) + j, step, stride=ROWS))
            return carry

        lax.fori_loop(0, length // step, turn, 0)

    def sweep(body, carry, unroll=8, reverse=False):
        def turn(i, carry):
            for u in range(unroll):
                token = i * unroll + u
                if reverse:
                    token = length - 1 - token
                carry = body(rows(token * ROWS, ROWS), carry)
            return carry

        return lax.fori_loop(0, length // unroll, turn, carry)

    def tree(terms):
        while len(terms) > 1:
            terms = [a + b for a, b in zip(terms[::2], terms[1::2])]
        return terms[0]

    loads[2].wait()
    loads[3].wait()

    def multiply(tokens, lanes, place):
        tokens_p[place, :] = inner_v[tokens, lanes].astype(F32) * signal_v[tokens, lanes].astype(F32)

    natural(multiply)

    decay = [mode(lam_s, m) for m in range(MODES)]

    def leave(token, state):
        p = tokens_p[token, :]
        return tuple(d * s + p for d, s in zip(decay, state))

    state = sweep(leave, (zero,) * MODES)
    sa.begin(state[:HALF])
    sb.begin(state[HALF:])
    pl.semaphore_wait(barrier, partners)
    sa.send()
    sb.send()

    for half, flow in enumerate((da, db)):
        some = range(half * HALF, half * HALF + HALF)
        decay8 = [mode(lam_s, m) for m in some]
        weight8 = [mode(wts_s, m) for m in some]

        def respond(token, carry, decay=decay8, weight=weight8, half=half):
            p = tokens_p[token, :]
            lagged = [d * (a + s) for d, a, s in zip(decay, carry[HALF:], carry[:HALF])]
            state = [d * s + p for d, s in zip(decay, carry[:HALF])]
            here = tree([w * s for w, s in zip(weight, state)])
            tokens_r[token, :] = here if half == 0 else tokens_r[token, :] + here
            return tuple(state + lagged)

        flow.begin(sweep(respond, (zero,) * MODES)[HALF:])

    sb.prefix()
    sa.total()
    db.send()
    da.send()
    sb.give_back()
    db.prefix()
    sa.prefix()
    sb.last_z()
    da.total()
    sa.give_back()
    db.give_back()
    da.prefix()

    loads[4].wait()
    loads[5].wait()
    loads[6].wait()
    gain_ref[...] = gain_v[...].astype(F32)[None, :]
    fade = []
    for m, value in enumerate(sa.arrived() + sb.arrived()):
        put(at["state_in"], m, value)
        fade.append(mode(wts_s, m) * value)

    def carried(token, fade):
        fade = tuple(d * f for d, f in zip(decay, fade))
        tokens_r[token, :] = tokens_r[token, :] + tree(list(fade))
        return fade

    sweep(carried, tuple(fade))

    def mix(i, carry):
        tokens = rows(i * 16, 16)
        squares = jnp.zeros((16, LANES), F32)
        inners = jnp.zeros((16, LANES), F32)
        for j in range(ROWS):
            lanes = slice(j * LANES, (j + 1) * LANES)
            mixed = outer_v[tokens, lanes].astype(F32) * tokens_r[pl.ds(i * 128 + j, 16, stride=ROWS), :]
            gained = cot_v[tokens, lanes].astype(F32) * gain_ref[:, lanes]
            mixed_n[tokens, lanes] = mixed
            squares = squares + mixed * mixed
            inners = inners + gained * mixed
        at["sums_a"][tokens, :] = squares
        at["sums_b"][tokens, :] = inners
        return carry

    lax.fori_loop(0, length // 16, mix, 0)

    def across(a, b):
        return lax.dot_general(
            a, b, (((1,), (1,)), ((), ())), precision=lax.Precision.HIGHEST,
            preferred_element_type=F32,
        )

    ones = jnp.ones((ROWS, LANES), F32)
    upper = lax.broadcasted_iota(jnp.int32, (ROWS, length), 0) < 4
    box_t[rows(t * ROWS, ROWS), :] = jnp.where(
        upper, across(ones, at["sums_a"][...]), across(ones, at["sums_b"][...])
    )
    norms.start()
    db.last_z()
    da.give_back()

    norms.wait()
    both = jnp.zeros((ROWS, length), F32)
    for q in range(nt):
        both = both + mode(box_t, q)
    scale = lax.rsqrt(both[0:1, :] / D + 1e-06)
    pull = scale * scale * scale * both[4:5, :] / D
    row_id = lax.broadcasted_iota(jnp.int32, (length, length), 0)
    col_id = lax.broadcasted_iota(jnp.int32, (length, length), 1)
    square = jnp.ones((LANES, length), F32)
    at["cols_a"][...] = across(jnp.where(row_id == col_id, scale, 0.0), square)
    at["cols_b"][...] = across(jnp.where(row_id == col_id, pull, 0.0), square)

    def finish(i, carry):
        tokens = rows(i * 16, 16)
        a, b = at["cols_a"][tokens, :], at["cols_b"][tokens, :]
        for j in range(ROWS):
            lanes = slice(j * LANES, (j + 1) * LANES)
            place = pl.ds(i * 128 + j, 16, stride=ROWS)
            mixed = mixed_n[tokens, lanes]
            gain = gain_ref[:, lanes]
            gained = cot_v[tokens, lanes].astype(F32) * gain
            grad = a * gained - mixed * b
            tokens_w[place, :] = grad * outer_v[tokens, lanes].astype(F32)
            output_ref[tokens, lanes] = (mixed * a * gain).astype(BF16)
            gouter_ref[tokens, lanes] = (grad * tokens_r[place, :]).astype(BF16)
        return carry

    lax.fori_loop(0, length // 16, finish, 0)

    def leave_back(token, adjoint):
        w = tokens_w[token, :]
        return tuple(d * a + w for d, a in zip(decay, adjoint))

    adjoint = sweep(leave_back, (zero,) * MODES, reverse=True)
    adjoint = [d * a for d, a in zip(decay, adjoint)]
    ga.begin(adjoint[:HALF])
    gb.begin(adjoint[HALF:])
    ga.send()
    gb.send()

    for m, value in enumerate(da.arrived() + db.arrived()):
        put(at["stated_in"], m, value)

    for half in range(2):
        some = range(half * HALF, half * HALF + HALF)
        decay8 = [mode(lam_s, m) for m in some]

        def correlate(token, carry, decay=decay8):
            p, w = tokens_p[token, :], tokens_w[token, :]
            state, lagged, first, second = carry[:8], carry[8:16], carry[16:24], carry[24:]
            lagged = [d * (a + s) for d, a, s in zip(decay, lagged, state)]
            state = [d * s + p for d, s in zip(decay, state)]
            first = [f + w * s for f, s in zip(first, state)]
            second = [f + w * a for f, a in zip(second, lagged)]
            return tuple(state + lagged + first + second)

        carry = sweep(
            correlate,
            tuple(mode(at["state_in"], m) for m in some)
            + tuple(mode(at["stated_in"], m) for m in some)
            + (zero,) * 16,
            unroll=4,
        )
        for i, m in enumerate(some):
            base = (m // 2) * pair + (m % 2) * ROWS
            prm_s[base : base + ROWS, :] = carry[16 + i]
            prm_s[base + pair // 2 : base + pair // 2 + ROWS, :] = carry[24 + i]
    prm_split.start()
    prm_y[rows(y * pair, pair), :] = prm_s[rows(y * pair, pair), :]

    def add_up(box, n):
        total = box[0:pair, :]
        for q in range(1, n):
            total = total + box[q * pair : (q + 1) * pair, :]
        return total

    gb.prefix()
    ga.total()

    for half in range(2):
        some = range(half * HALF, half * HALF + HALF)
        decay8 = [mode(lam_s, m) for m in some]
        weight8 = [mode(wts_s, m) for m in some]

        def pull_back(token, adjoint, decay=decay8, weight=weight8, half=half):
            w = tokens_w[token, :]
            adjoint = tuple(d * a + w for d, a in zip(decay, adjoint))
            here = tree([k * a for k, a in zip(weight, adjoint)])
            tokens_r[token, :] = here if half == 0 else tokens_r[token, :] + here
            return adjoint

        sweep(pull_back, (zero,) * HALF, reverse=True)

    gb.give_back()
    prm_split.wait()
    prm_x[rows(x * pair, pair), :] = add_up(prm_y, NY)
    prm_sum_x.start()
    ga.prefix()
    prm_sum_x.wait()
    prm_z[rows(z * pair, pair), :] = add_up(prm_x, NX)
    prm_sum_z.start()
    gb.last_z()
    ga.give_back()
    prm_sum_z.wait()
    prm_g[rows(y * pair, pair), :] = add_up(prm_z, nz)
    prm_back.start()

    fade = tuple(
        mode(wts_s, m) * value for m, value in enumerate(ga.arrived() + gb.arrived())
    )

    def carried_back(token, fade):
        tokens_r[token, :] = tokens_r[token, :] + tree(list(fade))
        return tuple(d * f for d, f in zip(decay, fade))

    sweep(carried_back, fade, reverse=True)

    def last(tokens, lanes, place):
        grad = tokens_r[place, :]
        ginner_ref[tokens, lanes] = (grad * signal_v[tokens, lanes].astype(F32)).astype(BF16)
        gsignal_ref[tokens, lanes] = (grad * inner_v[tokens, lanes].astype(F32)).astype(BF16)

    natural(last)

    prm_back.wait()
    whole = MODES * ROWS
    for m in range(MODES):
        base = (m // 2) * pair + (m % 2) * ROWS
        first = prm_g[base : base + ROWS, :]
        second = prm_g[base + pair // 2 : base + pair // 2 + ROWS, :]
        put(fin_s, m, factor * (mode(root_s, m) * first))
        put(fin_s, m, factor * (mode(wts_s, m) * (0.5 * first - mode(rho_s, m) * second)), whole)
    for half in range(MODES // 8):
        for j in range(ROWS):
            lanes = slice(j * LANES, (j + 1) * LANES)
            some = slice(half * 8, half * 8 + 8)
            rgrad_ref[some, lanes] = fin_s[pl.ds(half * 64 + j, 8, stride=ROWS), :]
            agrad_ref[some, lanes] = fin_s[pl.ds(whole + half * 64 + j, 8, stride=ROWS), :]
    for exchange in everything:
        exchange.drain()


def deliver(*refs):
    sem = refs[12]
    copies = [pltpu.make_async_copy(refs[i], refs[6 + i], sem.at[i]) for i in range(6)]
    for copy in copies:
        copy.start()
    for copy in copies:
        copy.wait()


def solution(mesh):
    nz, nt = mesh.shape["grp"], mesh.shape["tp"]
    blocks = mesh.shape["ctx"] * nz
    assert mesh.shape["ctx"] == NX * NY

    def step(outer_gate, inner_gate, signal, residues, log_rates, norm_gain, cotangent):
        length, channels = outer_gate.shape
        assert channels == ROWS * LANES and length == LANES and residues.shape[0] == MODES
        factor = 1.0 / math.sqrt(length * blocks)
        wide = pltpu.VMEM((length, channels), BF16)
        params = pltpu.VMEM(residues.shape, F32)
        exchanges = 7 * (2 * (NY - 1) + (NX - 1) + (nz - 1)) + (nt - 1)
        scratch = (
            [wide] * 4 + [params] * 2
            + [pltpu.VMEM((channels,), BF16), pltpu.VMEM((1, channels), F32), pltpu.VMEM((length, channels), F32)]
            + [
                pltpu.SemaphoreType.DMA((7,)),
                pltpu.SemaphoreType.DMA((exchanges,)),
                pltpu.SemaphoreType.DMA((exchanges,)),
            ]
            + [pltpu.VMEM((count, LANES), F32) for count in layout(nz, nt, length).values()]
        )
        vmem = pl.BlockSpec(memory_space=pltpu.VMEM)
        hbm = pl.BlockSpec(memory_space=pltpu.HBM)
        shapes = (jax.ShapeDtypeStruct((length, channels), BF16),) * 4 + (
            jax.ShapeDtypeStruct(residues.shape, F32),
        ) * 2

        def body(*refs):
            kernel(nz, nt, length, factor, *refs)

        results = pl.pallas_call(
            body,
            out_shape=shapes,
            in_specs=[hbm] * 7,
            out_specs=(vmem,) * 6,
            scratch_shapes=scratch,
            compiler_params=pltpu.CompilerParams(
                collective_id=0, has_side_effects=True, vmem_limit_bytes=40 * 1024 * 1024
            ),
            name="hyena",
        )(
            *(
                pltpu.with_memory_space_constraint(a, pltpu.HBM)
                for a in (outer_gate, inner_gate, signal, cotangent, residues, log_rates, norm_gain)
            )
        )
        return pl.pallas_call(
            deliver,
            out_shape=shapes,
            in_specs=[pl.BlockSpec(memory_space=pl.ANY)] * 6,
            out_specs=(hbm,) * 6,
            scratch_shapes=[pltpu.SemaphoreType.DMA((6,))],
            compiler_params=pltpu.CompilerParams(vmem_limit_bytes=4 * 1024 * 1024),
            name="deliver",
        )(*results)

    wide, narrow = P(("ctx", "grp"), "tp"), P(None, "tp")
    return jax.shard_map(
        step,
        mesh=mesh,
        in_specs=(wide, wide, wide, narrow, narrow, P("tp"), wide),
        out_specs=(wide,) * 4 + (narrow,) * 2,
        check_vma=False,
    )
```

time: 92.4 us -> 70.2 us (0.76)
  the two profiles are of different devices: /device:TPU:4 before, /device:TPU:8 now
where the time goes in v2:
time: 70.2 us; the launch traced here: 70.1 us
  Pallas kernels  69.4 us (99%)
    pallas_call x1, Pallas kernels, step(): pl.pallas_call(body, out_shape=shapes, in_specs=[hbm] * 7, out_specs=(vme...  68.4 us

profile of v2, /device:TPU:8, one launch (start us, length us, event | category | flops | bytes accessed | tf_op | source)
XLA Modules:
  0.0 70.1 jit_solution(7196532757883600772)
XLA Ops:
  0.6 68.4 %hyena.1 = (bf16[128,1024]{1,0:T(8,128)(2,1)S(1)}, bf16[128,1024]{1,0:T(8,128)(2,1)S(1)}, bf16[128,1024]{1,0:T(8,128)(2,1)S(1)}, bf16[128,1024]{1,0:T(8,128)(2,1...) custom-call(bf16[128,1024]{1,0:T(8,128)(2,1)} %refs_0_.1, bf16[128,1024]{1,0:T(8,128)(2,1)} %refs_1_.1, ...), custom_call_target="tpu_custom_call" | custom-call | tf_op jit(solution)/shard_map/hyena/pallas_call | solution.py:610
  69.0 1.1 %deliver.1 = (bf16[128,1024]{1,0:T(8,128)(2,1)}, bf16[128,1024]{1,0:T(8,128)(2,1)}, bf16[128,1024]{1,0:T(8,128)(2,1)}, bf16[128,1024]{1,0:T(8,128)(2,1)}, f32[16,1024]{1,0:T(8,128)}, /*index=5*/f32[16,1024]{1,0:T(8,128)}) custom-call(bf16[128,1024]{1,0:T(8,128)(2,1)S(1)} %get-tuple-element.12.refs_0_, bf16[128,1024]{1,0:T(8,128)(2,1)S(1)} %get-tuple-element.13.refs_1_, ...), custom_call_target="tpu_custom_call" | custom-call | tf_op jit(solution)/shard_map/deliver/pallas_call | solution.py:626

commit v3 on v2

--- a/solution.py
+++ b/solution.py
@@ -24,7 +24,7 @@
     shapes = {"tokens_p": length * ROWS, "tokens_r": length * ROWS, "tokens_w": length * ROWS}
     for name in ("sums_a", "sums_b", "cols_a", "cols_b"):
         shapes[name] = length
-    for name in ("rho_s", "root_s", "lam_s", "wts_s", "big_s", "state_in", "stated_in", "adj_in"):
+    for name in ("rho_s", "root_s", "lam_s", "wts_s", "big_s", "state_in"):
         shapes[name] = MODES * ROWS
     for flow in FLOWS:
         shapes |= {
@@ -32,11 +32,13 @@
             flow + ".tot": span, flow + ".pre": span, flow + ".box_y": NY * own,
             flow + ".box_x": NX * own, flow + ".ret": NY * own, flow + ".box_r": NY * own,
         }
-    pair = 4 * ROWS
-    shapes |= {
-        "prm_s": NY * pair, "prm_y": NY * pair, "prm_x": NX * pair, "prm_z": nz * pair,
-        "prm_g": NY * pair, "fin_s": 2 * MODES * ROWS, "box_t": nt * ROWS,
-    }
+    pair = 2 * ROWS
+    for half in ("p0", "p1"):
+        shapes |= {
+            half + ".sum": NY * pair, half + ".box_y": NY * pair, half + ".box_z": nz * pair,
+            half + ".box_x": NX * pair, half + ".all": NY * pair,
+        }
+    shapes |= {"tokens_g": length * ROWS, "fin_s": 2 * MODES * ROWS, "box_t": nt * ROWS}
     return shapes
 
 
@@ -50,7 +52,7 @@
     at = dict(zip(layout(nz, nt, length), scratch))
     tokens_p, tokens_r, tokens_w = at["tokens_p"], at["tokens_r"], at["tokens_w"]
     rho_s, root_s, lam_s, wts_s, big_s = (at[k] for k in ("rho_s", "root_s", "lam_s", "wts_s", "big_s"))
-    prm_s, prm_y, prm_x, prm_z, prm_g = (at[k] for k in ("prm_s", "prm_y", "prm_x", "prm_z", "prm_g"))
+    tokens_g = at["tokens_g"]
     box_t, fin_s = at["box_t"], at["fin_s"]
 
     ctx = lax.axis_index("ctx")
@@ -69,7 +71,6 @@
         "t": (nt, t, lambda q: {"tp": q}),
     }
     used = [0]
-    everything = []
 
     class Exchange:
         def __init__(self, axis, box, size, piece=None):
@@ -79,7 +80,6 @@
             self.first = used[0]
             used[0] += self.n - 1
             self.far_first = sorted(range(1, self.n), key=lambda k: -min(k, self.n - k))
-            everything.append(self)
 
         def slot(self, q):
             return self.box.at[rows(q * self.size, self.size)]
@@ -261,12 +261,41 @@
     sa, sb = Flow("s_first", True, True), Flow("s_last", False, True)
     da, db = Flow("d_first", True, True, sa), Flow("d_last", False, True, sb)
     ga, gb = Flow("g_first", True, False), Flow("g_last", False, False)
-    pair = 4 * ROWS
     norms = Exchange("t", box_t, ROWS)
-    prm_split = Exchange("y", prm_y, pair, lambda q: prm_s.at[rows(q * pair, pair)])
-    prm_sum_x = Exchange("x", prm_x, pair)
-    prm_sum_z = Exchange("z", prm_z, pair)
-    prm_back = Exchange("y", prm_g, pair)
+    pair = 2 * ROWS
+
+    class Total:
+        def __init__(self, name):
+            for key in ("sum", "box_y", "box_z", "box_x", "all"):
+                setattr(self, key, at[name + "." + key])
+            self.ex_y = Exchange("y", self.box_y, pair, lambda q: self.sum.at[rows(q * pair, pair)])
+            self.ex_z = Exchange("z", self.box_z, pair)
+            self.ex_x = Exchange("x", self.box_x, pair)
+            self.ex_all = Exchange("y", self.all, pair)
+
+        def split(self):
+            self.ex_y.start()
+            here = rows(y * pair, pair)
+            self.box_y[here, :] = self.sum[here, :]
+
+        def hand_on(self, exchange, following):
+            exchange.wait()
+            total = exchange.box[0:pair, :]
+            for q in range(1, exchange.n):
+                total = total + exchange.box[q * pair : (q + 1) * pair, :]
+            following.box[rows(following.me * pair, pair), :] = total
+            following.start()
+
+        def over_z(self):
+            self.hand_on(self.ex_y, self.ex_z)
+
+        def over_x(self):
+            self.hand_on(self.ex_z, self.ex_x)
+
+        def to_all(self):
+            self.hand_on(self.ex_x, self.ex_all)
+
+    totals = (Total("p0"), Total("p1"))
 
     loads = [
         pltpu.make_async_copy(src, dst, in_sem.at[i])
@@ -411,12 +440,20 @@
     lax.fori_loop(0, length // 16, mix, 0)
 
     def across(a, b):
-        return lax.dot_general(
-            a, b, (((1,), (1,)), ((), ())), precision=lax.Precision.HIGHEST,
-            preferred_element_type=F32,
+        ones_first = a.dtype == BF16
+        left, parts = (b if ones_first else a), []
+        for _ in range(3):
+            parts.append(left.astype(BF16))
+            left = left - parts[-1].astype(F32)
+        return sum(
+            lax.dot_general(
+                *((a, part) if ones_first else (part, b)), (((1,), (1,)), ((), ())),
+                preferred_element_type=F32,
+            )
+            for part in reversed(parts)
         )
 
-    ones = jnp.ones((ROWS, LANES), F32)
+    ones = jnp.ones((ROWS, LANES), BF16)
     upper = lax.broadcasted_iota(jnp.int32, (ROWS, length), 0) < 4
     box_t[rows(t * ROWS, ROWS), :] = jnp.where(
         upper, across(ones, at["sums_a"][...]), across(ones, at["sums_b"][...])
@@ -433,7 +470,7 @@
     pull = scale * scale * scale * both[4:5, :] / D
     row_id = lax.broadcasted_iota(jnp.int32, (length, length), 0)
     col_id = lax.broadcasted_iota(jnp.int32, (length, length), 1)
-    square = jnp.ones((LANES, length), F32)
+    square = jnp.ones((LANES, length), BF16)
     at["cols_a"][...] = across(jnp.where(row_id == col_id, scale, 0.0), square)
     at["cols_b"][...] = across(jnp.where(row_id == col_id, pull, 0.0), square)
 
@@ -448,25 +485,32 @@
             gained = cot_v[tokens, lanes].astype(F32) * gain
             grad = a * gained - mixed * b
             tokens_w[place, :] = grad * outer_v[tokens, lanes].astype(F32)
+        return carry
+
+    lax.fori_loop(0, length // 16, finish, 0)
+
+    def outputs(i, carry):
+        tokens = rows(i * 16, 16)
+        a, b = at["cols_a"][tokens, :], at["cols_b"][tokens, :]
+        for j in range(ROWS):
+            lanes = slice(j * LANES, (j + 1) * LANES)
+            mixed = mixed_n[tokens, lanes]
+            gain = gain_ref[:, lanes]
+            gained = cot_v[tokens, lanes].astype(F32) * gain
+            grad = a * gained - mixed * b
+            response = tokens_r[pl.ds(i * 128 + j, 16, stride=ROWS), :]
             output_ref[tokens, lanes] = (mixed * a * gain).astype(BF16)
-            gouter_ref[tokens, lanes] = (grad * tokens_r[place, :]).astype(BF16)
+            gouter_ref[tokens, lanes] = (grad * response).astype(BF16)
         return carry
 
-    lax.fori_loop(0, length // 16, finish, 0)
+    late = [mode(lam_s, m) for m in range(HALF, MODES)]
 
     def leave_back(token, adjoint):
         w = tokens_w[token, :]
-        return tuple(d * a + w for d, a in zip(decay, adjoint))
-
-    adjoint = sweep(leave_back, (zero,) * MODES, reverse=True)
-    adjoint = [d * a for d, a in zip(decay, adjoint)]
-    ga.begin(adjoint[:HALF])
-    gb.begin(adjoint[HALF:])
-    ga.send()
+        return tuple(d * a + w for d, a in zip(late, adjoint))
+
+    gb.begin([d * a for d, a in zip(late, sweep(leave_back, (zero,) * HALF, reverse=True))])
     gb.send()
-
-    for m, value in enumerate(da.arrived() + db.arrived()):
-        put(at["stated_in"], m, value)
 
     for half in range(2):
         some = range(half * HALF, half * HALF + HALF)
@@ -474,35 +518,32 @@
 
         def correlate(token, carry, decay=decay8):
             p, w = tokens_p[token, :], tokens_w[token, :]
-            state, lagged, first, second = carry[:8], carry[8:16], carry[16:24], carry[24:]
-            lagged = [d * (a + s) for d, a, s in zip(decay, lagged, state)]
-            state = [d * s + p for d, s in zip(decay, state)]
-            first = [f + w * s for f, s in zip(first, state)]
-            second = [f + w * a for f, a in zip(second, lagged)]
-            return tuple(state + lagged + first + second)
-
-        carry = sweep(
-            correlate,
-            tuple(mode(at["state_in"], m) for m in some)
-            + tuple(mode(at["stated_in"], m) for m in some)
-            + (zero,) * 16,
-            unroll=4,
-        )
+            adjoint, lagged, first, second = carry[:8], carry[8:16], carry[16:24], carry[24:]
+            lagged = [d * (b + a) for d, b, a in zip(decay, lagged, adjoint)]
+            adjoint = [d * a + w for d, a in zip(decay, adjoint)]
+            first = [f + p * a for f, a in zip(first, adjoint)]
+            second = [f + p * b for f, b in zip(second, lagged)]
+            return tuple(adjoint + lagged + first + second)
+
+        carry = sweep(correlate, (zero,) * 32, unroll=4, reverse=True)
+        leaving = [d * a for d, a in zip(decay8, carry[:8])]
+        leaving_lagged = [d * (b + a) for d, b, a in zip(decay8, carry[8:16], carry[:8])]
+        if half == 0:
+            ga.begin(leaving)
+            ga.send()
+        lagged_in = (da, db)[half].arrived()
         for i, m in enumerate(some):
-            base = (m // 2) * pair + (m % 2) * ROWS
-            prm_s[base : base + ROWS, :] = carry[16 + i]
-            prm_s[base + pair // 2 : base + pair // 2 + ROWS, :] = carry[24 + i]
-    prm_split.start()
-    prm_y[rows(y * pair, pair), :] = prm_s[rows(y * pair, pair), :]
-
-    def add_up(box, n):
-        total = box[0:pair, :]
-        for q in range(1, n):
-            total = total + box[q * pair : (q + 1) * pair, :]
-        return total
+            start = mode(at["state_in"], m)
+            put(totals[half].sum, 2 * i, carry[16 + i] + leaving[i] * start)
+            put(totals[half].sum, 2 * i + 1,
+                carry[24 + i] + leaving_lagged[i] * start + leaving[i] * lagged_in[i])
+        totals[half].split()
 
     gb.prefix()
+    totals[0].over_z()
+    gb.give_back()
     ga.total()
+    totals[1].over_z()
 
     for half in range(2):
         some = range(half * HALF, half * HALF + HALF)
@@ -513,48 +554,47 @@
             w = tokens_w[token, :]
             adjoint = tuple(d * a + w for d, a in zip(decay, adjoint))
             here = tree([k * a for k, a in zip(weight, adjoint)])
-            tokens_r[token, :] = here if half == 0 else tokens_r[token, :] + here
+            tokens_g[token, :] = here if half == 0 else tokens_g[token, :] + here
             return adjoint
 
         sweep(pull_back, (zero,) * HALF, reverse=True)
 
-    gb.give_back()
-    prm_split.wait()
-    prm_x[rows(x * pair, pair), :] = add_up(prm_y, NY)
-    prm_sum_x.start()
+    totals[0].over_x()
+    gb.last_z()
     ga.prefix()
-    prm_sum_x.wait()
-    prm_z[rows(z * pair, pair), :] = add_up(prm_x, NX)
-    prm_sum_z.start()
-    gb.last_z()
+    totals[1].over_x()
+    totals[0].to_all()
     ga.give_back()
-    prm_sum_z.wait()
-    prm_g[rows(y * pair, pair), :] = add_up(prm_z, nz)
-    prm_back.start()
+    lax.fori_loop(0, length // 16, outputs, 0)
+    totals[1].to_all()
+    for flow in (sa, sb, da, db):
+        for exchange in (flow.ex_z, flow.ex_y, flow.ex_x, flow.ex_r):
+            exchange.drain()
+    norms.drain()
 
     fade = tuple(
         mode(wts_s, m) * value for m, value in enumerate(ga.arrived() + gb.arrived())
     )
 
     def carried_back(token, fade):
-        tokens_r[token, :] = tokens_r[token, :] + tree(list(fade))
+        tokens_g[token, :] = tokens_g[token, :] + tree(list(fade))
         return tuple(d * f for d, f in zip(decay, fade))
 
     sweep(carried_back, fade, reverse=True)
 
     def last(tokens, lanes, place):
-        grad = tokens_r[place, :]
+        grad = tokens_g[place, :]
         ginner_ref[tokens, lanes] = (grad * signal_v[tokens, lanes].astype(F32)).astype(BF16)
         gsignal_ref[tokens, lanes] = (grad * inner_v[tokens, lanes].astype(F32)).astype(BF16)
 
     natural(last)
 
-    prm_back.wait()
     whole = MODES * ROWS
     for m in range(MODES):
-        base = (m // 2) * pair + (m % 2) * ROWS
-        first = prm_g[base : base + ROWS, :]
-        second = prm_g[base + pair // 2 : base + pair // 2 + ROWS, :]
+        if m % HALF == 0:
+            totals[m // HALF].ex_all.wait()
+        first = mode(totals[m // HALF].all, 2 * (m % HALF))
+        second = mode(totals[m // HALF].all, 2 * (m % HALF) + 1)
         put(fin_s, m, factor * (mode(root_s, m) * first))
         put(fin_s, m, factor * (mode(wts_s, m) * (0.5 * first - mode(rho_s, m) * second)), whole)
     for half in range(MODES // 8):
@@ -563,8 +603,12 @@
             some = slice(half * 8, half * 8 + 8)
             rgrad_ref[some, lanes] = fin_s[pl.ds(half * 64 + j, 8, stride=ROWS), :]
             agrad_ref[some, lanes] = fin_s[pl.ds(whole + half * 64 + j, 8, stride=ROWS), :]
-    for exchange in everything:
-        exchange.drain()
+    for flow in (ga, gb):
+        for exchange in (flow.ex_z, flow.ex_y, flow.ex_x, flow.ex_r):
+            exchange.drain()
+    for total in totals:
+        for exchange in (total.ex_y, total.ex_z, total.ex_x, total.ex_all):
+            exchange.drain()
 
 
 def deliver(*refs):
@@ -587,7 +631,7 @@
         factor = 1.0 / math.sqrt(length * blocks)
         wide = pltpu.VMEM((length, channels), BF16)
         params = pltpu.VMEM(residues.shape, F32)
-        exchanges = 7 * (2 * (NY - 1) + (NX - 1) + (nz - 1)) + (nt - 1)
+        exchanges = 8 * (2 * (NY - 1) + (NX - 1) + (nz - 1)) + (nt - 1)
         scratch = (
             [wide] * 4 + [params] * 2
             + [pltpu.VMEM((channels,), BF16), pltpu.VMEM((1, channels), F32), pltpu.VMEM((length, channels), F32)]

time: 70.2 us -> 68.8 us (0.980)
  Pallas kernels: 69.4 us -> 68 us
    pallas_call x1, Pallas kernels: 68.4 us -> 66.9 us  [step(): pl.pallas_call(body, out_shape=shapes, in_specs=[hbm] * 7, out_specs=(vme...]
where the time goes in v3:
time: 68.8 us; the launch traced here: 68.6 us
  Pallas kernels  68 us (99%)
    pallas_call x1, Pallas kernels, step(): pl.pallas_call(body, out_shape=shapes, in_specs=[hbm] * 7, out_specs=(vme...  66.9 us

profile of v3, /device:TPU:8, one launch (start us, length us, event | category | flops | bytes accessed | tf_op | source)
XLA Modules:
  0.0 68.6 jit_solution(655495205739907498)
XLA Ops:
  0.6 66.9 %hyena.1 = (bf16[128,1024]{1,0:T(8,128)(2,1)S(1)}, bf16[128,1024]{1,0:T(8,128)(2,1)S(1)}, bf16[128,1024]{1,0:T(8,128)(2,1)S(1)}, bf16[128,1024]{1,0:T(8,128)(2,1...) custom-call(bf16[128,1024]{1,0:T(8,128)(2,1)} %refs_0_.1, bf16[128,1024]{1,0:T(8,128)(2,1)} %refs_1_.1, ...), custom_call_target="tpu_custom_call" | custom-call | tf_op jit(solution)/shard_map/hyena/pallas_call | solution.py:654
  67.6 1.1 %deliver.1 = (bf16[128,1024]{1,0:T(8,128)(2,1)}, bf16[128,1024]{1,0:T(8,128)(2,1)}, bf16[128,1024]{1,0:T(8,128)(2,1)}, bf16[128,1024]{1,0:T(8,128)(2,1)}, f32[16,1024]{1,0:T(8,128)}, /*index=5*/f32[16,1024]{1,0:T(8,128)}) custom-call(bf16[128,1024]{1,0:T(8,128)(2,1)S(1)} %get-tuple-element.12.refs_0_, bf16[128,1024]{1,0:T(8,128)(2,1)S(1)} %get-tuple-element.13.refs_1_, ...), custom_call_target="tpu_custom_call" | custom-call | tf_op jit(solution)/shard_map/deliver/pallas_call | solution.py:670
